TPU v7x, 32 devices: a whole 2x2x4 slice. The times are simulated.
32 devices in a mesh: beam: 2 (over y), freq: 8 (over z, x), tm: 2 (over core).
Axes of the slice: x: 2, y: 2, z: 4, core: 2. Of those that a mesh axis runs over, the one named last changes fastest.
Arguments:
- spectra: float32 [256, 16384], P(('beam', 'freq'), 'tm'), parts along dimension 0, may hold values from -250 to 250
- local_delays: int32 [4, 3, 128], P(None, None, 'freq'), may hold values from 0 to 8, as said below
- merge_delays: int32 [3, 3, 128], P(None, None, 'freq'), may hold values from 0 to 64, as said below
- widths: int32 [16], replicated, may hold values from 1 to 32, as said below
Outputs:
- detections: float32 [256, 16384], P(('beam', 'freq'), 'tm'), parts along dimension 0
There are 2 independent parts, one for each index of `beam`. A program takes and returns all parts, laid end to end along the dimension named above; an argument that names none is the same for every part. Nothing has to cross between parts.
Inputs may be any that keep to these rules, and one draw needn't show every extreme that they name: `local_delays`: entries [s, 0, r] and [s, 1, r] lie in 0 to 2**s - 1, entry [s, 2, r] in 0 to 2**s, and [s, 2, 0] equals 2**s. `merge_delays`: entries [j, 0, r] and [j, 1, r] lie in 0 to 15, entry [j, 2, r] in 0 to 16 * 2**j, and [j, 2, 0] equals 16 * 2**j. 16 distinct widths, one of them 32.
All inputs are finite; a program needn't handle non-finite values.
Results may differ from a plain program's by a relative error of at most 0.00002.
Values sent between devices are 32-bit elements; how exact they have to be, the bound alone decides.
A program may use at most 64 MiB of HBM per device.

v0:
```python
import math

import jax
import jax.numpy as jnp
from jax import lax
from jax.sharding import PartitionSpec as P

WMAX = 32


EPSILON = 1e-05


def from_behind(value, axis, by):
    size = lax.axis_size(axis)
    pairs = [(i, i + by) for i in range(size) if 0 <= i + by < size]
    return lax.ppermute(value, axis, pairs)


def partner_2(value, axis, bit):
    mask = 2**bit
    pairs = [(source, source ^ mask) for source in range(lax.axis_size(axis))]
    return lax.ppermute(value, axis, pairs)


def shift_rows(signal, delays, length, largest):
    bit_count = largest.bit_length()
    needed = length + 2**bit_count - 1
    current = jnp.pad(signal, ((0, 0), (0, max(0, needed - signal.shape[1]))))
    for bit_num in reversed(range(bit_count)):
        step = 2**bit_num
        new_len = length + step - 1
        taken = (delays // step % 2 == 1)[:, None]
        current = jnp.where(taken, current[:, step : step + new_len], current[:, :new_len])
    return current


def per_device(spectra, local_delays, merge_delays, widths):
    channels, block_len = spectra.shape
    sample_total = block_len * lax.axis_size("tm")
    freq_count = lax.axis_size("freq")
    totals = lax.psum(jnp.sum(spectra, axis=1, keepdims=True), "tm")
    centered = spectra - totals / sample_total
    spread = lax.psum(jnp.sum(centered * centered, axis=1, keepdims=True), "tm")
    series = centered / jnp.sqrt(spread / sample_total + EPSILON)
    reach = channels * freq_count - 1 + WMAX - 1
    leading = from_behind(series[:, :reach], "tm", -1)
    series = jnp.concatenate([series, leading], axis=1)
    row_ids = jnp.arange(channels, dtype=jnp.int32)
    for level_num in range(channels.bit_length() - 1):
        level_size = 2**level_num
        base_row = row_ids // (2 * level_size) * (2 * level_size)
        low_rows = series[base_row + local_delays[level_num, 0]]
        high_rows = series[base_row + level_size + local_delays[level_num, 1]]
        keep_len = series.shape[1] - level_size
        series = low_rows[:, :keep_len] + shift_rows(
            high_rows, local_delays[level_num, 2], keep_len, level_size
        )
    for level_num in range(freq_count.bit_length() - 1):
        stride = 2**level_num
        span = channels * stride
        is_upper = lax.axis_index("freq") // stride % 2 == 1
        low_pick = merge_delays[level_num, 0]
        high_pick = merge_delays[level_num, 1]
        partner = partner_2(series, "freq", level_num)
        low_rows = jnp.where(is_upper, partner[low_pick], series[low_pick])
        high_rows = jnp.where(is_upper, series[high_pick], partner[high_pick])
        keep_len = series.shape[1] - span
        series = low_rows[:, :keep_len] + shift_rows(
            high_rows, merge_delays[level_num, 2], keep_len, span
        )
    running = jnp.zeros((channels, block_len), jnp.float32)
    strongest = jnp.full((channels, block_len), -jnp.inf, jnp.float32)
    for offset in range(WMAX):
        running = running + series[:, offset : offset + block_len]
        chosen = jnp.any(widths == offset + 1)
        strongest = jnp.where(
            chosen, jnp.maximum(strongest, running * (1.0 / math.sqrt(offset + 1))), strongest
        )
    return strongest * (1.0 / math.sqrt(channels * freq_count))


def solution(mesh):
    placed = (P(("beam", "freq"), "tm"), P(None, None, "freq"), P(None, None, "freq"), P())
    return jax.shard_map(
        per_device, mesh=mesh, in_specs=placed, out_specs=P(("beam", "freq"), "tm"), check_vma=False
    )
```

profile of v0, /device:TPU:0, one launch (start us, length us, event | category | flops | bytes accessed | tf_op | source)
XLA Modules:
  0.0 106.1 jit_solution(16173300033060606930)
XLA Ops:
  0.0 1.3 %reduce_sum.18 = f32[16]{0:T(128)S(1)} reduce(f32[16,8192]{1,0:T(8,128)} %param.4, f32[]{:T(128)} %constant.554.clone.1), dimensions={1}, to_apply=%region_32.33 | reduce | flops 131056 | bytes 524356 | tf_op jit(solution)/shard_map/reduce_sum | solution.py:42
  1.3 2.6 %psum.14 = f32[16,1]{0,1:T(1,128)S(1)} all-reduce(f32[16,1]{0,1:T(1,128)S(1)} %bitcast.265), channel_id=1, replica_groups=mesh['beam'=2,'freq'=8,'tm'=2] {'tm'}, use_global_device_ids=true, to_apply=%region_33.34 | all-reduce | flops 16 | bytes 128 | tf_op jit(solution)/shard_map/psum | solution.py:42
  4.2 2.5 %psum.15 = f32[16,1]{0,1:T(1,128)S(1)} all-reduce(f32[16,1]{0,1:T(1,128)S(1)} %bitcast.266), channel_id=1, replica_groups=mesh['beam'=2,'freq'=8,'tm'=2] {'tm'}, use_global_device_ids=true, to_apply=%region_35.36 | all-reduce | flops 16 | bytes 128 | tf_op jit(solution)/shard_map/psum | solution.py:44
  6.8 1.3 %collective-permute-start = (f32[16,158]{1,0:T(8,128)S(1)}, f32[16,158]{1,0:T(8,128)S(1)}, u32[]{:S(2)}, u32[]{:S(2)}) collective-permute-start(f32[16,158]{1,0:T(8,128)S(1)} %slice.514), channel_id=1, source_target_pairs={{1,0},{3,2},{5,4},{7,6},{9,8},{11,10},{13,12},{15,14},{17,16},{19,... | collective-permute-start | bytes 30344 | tf_op jit(solution)/shard_map/ppermute | solution.py:17
  8.3 1.6 %collective-permute-done = f32[16,158]{1,0:T(8,128)S(1)} collective-permute-done((f32[16,158]{1,0:T(8,128)S(1)}, f32[16,158]{1,0:T(8,128)S(1)}, u32[]{:S(2)}, u32[]{:S(2)}) %collective-permute-start) | collective-permute-done | bytes 10144 | tf_op jit(solution)/shard_map/ppermute | solution.py:17
  9.9 0.7 gather_fusion
  10.7 0.7 gather_fusion.1
  11.6 0.7 gather_fusion.3
  12.4 0.7 gather_fusion.2
  13.5 0.7 gather_fusion.5
  14.3 0.7 gather_fusion.4
  15.6 0.7 gather_fusion.7
  16.4 0.7 gather_fusion.6
  18.0 2.9 %collective-permute-start.1 = (f32[16,8335]{1,0:T(8,128)S(1)}, f32[16,8335]{1,0:T(8,128)S(1)}, u32[]{:S(2)}, u32[]{:S(2)}) collective-permute-start(f32[16,8335]{1,0:T(8,128)S(1)} %fusion), channel_id=1, source_target_pairs={{0,2},{2,0},{4,6},{6,4},{8,10},{10,8},{12,14},{14,12},{1,3},{3,1},... | collective-permute-start | bytes 1600328 | tf_op jit(solution)/shard_map/ppermute | solution.py:23
  21.0 0.7 gather_fusion.10
  21.7 0.7 gather_fusion.9
  22.4 11.0 %collective-permute-done.1 = f32[16,8335]{1,0:T(8,128)S(1)} collective-permute-done((f32[16,8335]{1,0:T(8,128)S(1)}, f32[16,8335]{1,0:T(8,128)S(1)}, u32[]{:S(2)}, u32[]{:S(2)}) %collective-permute-start.1) | collective-permute-done | bytes 533472 | tf_op jit(solution)/shard_map/ppermute | solution.py:23
  33.5 0.7 gather_fusion.11
  35.1 0.7 gather_fusion.8
  36.1 1.9 %collective-permute-start.2 = (f32[16,8319]{1,0:T(8,128)S(1)}, f32[16,8319]{1,0:T(8,128)S(1)}, u32[]{:S(2)}, u32[]{:S(2)}) collective-permute-start(f32[16,8319]{1,0:T(8,128)S(1)} %fusion.8), channel_id=1, source_target_pairs={{0,4},{2,6},{4,0},{6,2},{8,12},{10,14},{12,8},{14,10},{1,5},{3,7},... | collective-permute-start | bytes 1597256 | tf_op jit(solution)/shard_map/ppermute | solution.py:23
  38.0 0.7 gather_fusion.14
  38.7 0.7 gather_fusion.13
  39.4 10.3 %collective-permute-done.2 = f32[16,8319]{1,0:T(8,128)S(1)} collective-permute-done((f32[16,8319]{1,0:T(8,128)S(1)}, f32[16,8319]{1,0:T(8,128)S(1)}, u32[]{:S(2)}, u32[]{:S(2)}) %collective-permute-start.2) | collective-permute-done | bytes 532448 | tf_op jit(solution)/shard_map/ppermute | solution.py:23
  49.7 0.7 gather_fusion.15
  51.6 0.7 gather_fusion.12
  52.5 2.6 %collective-permute-start.3 = (f32[16,8287]{1,0:T(8,128)S(1)}, f32[16,8287]{1,0:T(8,128)S(1)}, u32[]{:S(2)}, u32[]{:S(2)}) collective-permute-start(f32[16,8287]{1,0:T(8,128)S(1)} %fusion.7), channel_id=1, source_target_pairs={{0,8},{2,10},{4,12},{6,14},{8,0},{10,2},{12,4},{14,6},{1,9},{3,11}... | collective-permute-start | bytes 1591112 | tf_op jit(solution)/shard_map/ppermute | solution.py:23
  55.8 1.2 %compare_reduce_fusion.31 = (pred[]{:T(512)}, pred[]{:T(512)}, pred[]{:T(512)}, pred[]{:T(512)}, pred[]{:T(512)}, /*index=5*/pred[]{:T(512)}, pred[]{:T(512)}, p...) fusion(s32[16]{0:T(128)S(1)} %copy-done.3), kind=kLoop, calls=%fused_computation.286 | loop fusion | flops 992 | bytes 96 | tf_op jit(solution)/shard_map/reduce_or | solution.py:76
  57.8 0.7 gather_fusion.17
  58.5 19.1 %collective-permute-done.3 = f32[16,8287]{1,0:T(8,128)S(1)} collective-permute-done((f32[16,8287]{1,0:T(8,128)S(1)}, f32[16,8287]{1,0:T(8,128)S(1)}, u32[]{:S(2)}, u32[]{:S(2)}) %collective-permute-start.3) | collective-permute-done | bytes 530400 | tf_op jit(solution)/shard_map/ppermute | solution.py:23
  77.6 0.7 gather_fusion.19
  79.7 0.7 gather_fusion.16
  80.7 25.4 %fusion.9 = f32[16,8192]{1,0:T(8,128)} fusion(f32[16,8223]{1,0:T(8,128)S(1)} %fusion.6, pred[]{:T(512)} %get-tuple-element.35, pred[]{:T(512)} %get-tuple-element.36, pred[]{:T(512)} %get-tuple-element.6, pred[]{:T(512)} %get-tuple-element.7, pred[]{:T(512)} %get-tuple-element.8, pred[]{:T(512)} %get-tuple-element.9, pred[]{:T(512)} %get-tuple-element.10, ...), kind=kLoop, calls=%fused_computation.92 | loop fusion | flops 16515072 | bytes 17301536 | tf_op jit(solution)/shard_map/mul | solution.py:80
  (58 shorter events, 8.0 us)
Async XLA Ops:
  0.0 3.9 %copy-start = (f32[16,8192]{1,0:T(8,128)S(1)}, f32[16,8192]{1,0:T(8,128)}, u32[]{:S(2)}) copy-start(f32[16,8192]{1,0:T(8,128)} %param.4) | copy-start | bytes 1572868
  6.8 1.3 %copy-start.1 = (s32[4,3,16]{2,0,1:T(4,128)S(1)}, s32[4,3,16]{2,0,1:T(4,128)}, u32[]{:S(2)}) copy-start(s32[4,3,16]{2,0,1:T(4,128)} %param.5) | copy-start | bytes 2308
  6.8 3.1 %collective-permute-start = (f32[16,158]{1,0:T(8,128)S(1)}, f32[16,158]{1,0:T(8,128)S(1)}, u32[]{:S(2)}, u32[]{:S(2)}) collective-permute-start(f32[16,158]{1,0:T(8,128)S(1)} %slice.514), channel_id=1, source_target_pairs={{1,0},{3,2},{5,4},{7,6},{9,8},{11,10},{13,12},{15,14},{17,16},{19,... | collective-permute-start | bytes 30344 | tf_op jit(solution)/shard_map/ppermute | solution.py:17
  17.8 3.1 %copy-start.2 = (s32[3,3,16]{2,1,0:T(4,128)S(1)}, s32[3,3,16]{2,1,0:T(4,128)}, u32[]{:S(2)}) copy-start(s32[3,3,16]{2,1,0:T(4,128)} %param.6) | copy-start | bytes 1732
  18.0 15.5 %collective-permute-start.1 = (f32[16,8335]{1,0:T(8,128)S(1)}, f32[16,8335]{1,0:T(8,128)S(1)}, u32[]{:S(2)}, u32[]{:S(2)}) collective-permute-start(f32[16,8335]{1,0:T(8,128)S(1)} %fusion), channel_id=1, source_target_pairs={{0,2},{2,0},{4,6},{6,4},{8,10},{10,8},{12,14},{14,12},{1,3},{3,1},... | collective-permute-start | bytes 1600328 | tf_op jit(solution)/shard_map/ppermute | solution.py:23
  36.1 13.7 %collective-permute-start.2 = (f32[16,8319]{1,0:T(8,128)S(1)}, f32[16,8319]{1,0:T(8,128)S(1)}, u32[]{:S(2)}, u32[]{:S(2)}) collective-permute-start(f32[16,8319]{1,0:T(8,128)S(1)} %fusion.8), channel_id=1, source_target_pairs={{0,4},{2,6},{4,0},{6,2},{8,12},{10,14},{12,8},{14,10},{1,5},{3,7},... | collective-permute-start | bytes 1597256 | tf_op jit(solution)/shard_map/ppermute | solution.py:23
  52.5 25.1 %collective-permute-start.3 = (f32[16,8287]{1,0:T(8,128)S(1)}, f32[16,8287]{1,0:T(8,128)S(1)}, u32[]{:S(2)}, u32[]{:S(2)}) collective-permute-start(f32[16,8287]{1,0:T(8,128)S(1)} %fusion.7), channel_id=1, source_target_pairs={{0,8},{2,10},{4,12},{6,14},{8,0},{10,2},{12,4},{14,6},{1,9},{3,11}... | collective-permute-start | bytes 1591112 | tf_op jit(solution)/shard_map/ppermute | solution.py:23
  55.2 0.7 copy-start.3
where the time goes:
time: 107 us; the launch traced here: 106 us
  waiting for transfers between devices  42.1 us (39%)
  other arithmetic  34.5 us (32%)
  local copies, waits for them, and re-layouts  15.3 us (14%)
  starting transfers between devices  8.67 us (8%)
  blocking collectives  5.09 us (5%)
    ppermute x3, waiting for transfers between devices, partner_2(): return lax.ppermute(value, axis, pairs)  40.5 us
    mul x1, other arithmetic, per_device(): return strongest * (1.0 / math.sqrt(channels * freq_count))  25.4 us
    ppermute x3, starting transfers between devices, partner_2(): return lax.ppermute(value, axis, pairs)  7.38 us
    gather x6, local copies, waits for them, and re-layouts, per_device(): low_rows = jnp.where(is_upper, partner[low_pick], series[low_pick])  4.39 us
    gather x6, local copies, waits for them, and re-layouts, per_device(): high_rows = jnp.where(is_upper, series[high_pick], partner[high_pick])  4.38 us
    select_n x21, other arithmetic, shift_rows(): jnp.where(taken, current[:, step:step + new_len], current[:, :new_len])  4.32 us
    gather x4, local copies, waits for them, and re-layouts, per_device(): high_rows = series[base_row + level_size + local_delays[level_num, 1]]  2.93 us
    gather x4, local copies, waits for them, and re-layouts, per_device(): low_rows = series[base_row + local_delays[level_num, 0]]  2.93 us
  transfers between devices with their start and end apart: 4, of which 4 were waited for; matrix products, arithmetic and copies ran while one was open for 5% of the time, Pallas kernels for 0%

commit v1 on v0

v1 whole, which is shorter than its diff:
```python
import functools
import math

import jax
import jax.numpy as jnp
from jax import lax
from jax.experimental import pallas as pl
from jax.experimental.pallas import tpu as pltpu
from jax.sharding import PartitionSpec as P

WMAX = 32
EPSILON = 1e-05
LANES = 128
SUB = 8
MESH = pl.DeviceIdType.MESH
FIRST_LAG = 1
MID_LAG = 1
LAST_LAG = 3


def kernel(geo, x_ref, ld_ref, md_ref, w_ref, o_ref, *scratch):
    channels, chunks, freq_count, halo_chunks, tile = geo
    groups = channels // SUB
    llevels = channels.bit_length() - 1
    flevels = freq_count.bit_length() - 1
    samples = chunks * LANES
    nwidth = w_ref.shape[0]
    halo, st_own, st_peer, nrm, fin, eb, tri, scl = scratch[:8]
    loc = scratch[8 : 8 + llevels]
    count = chunks // tile
    flat_bufs = scratch[8 + llevels : 8 + llevels + flevels * count]
    bufs = [flat_bufs[j * count : (j + 1) * count] for j in range(flevels)]
    hsend, hrecv, ssend, srecv, bsend, brecv = scratch[8 + llevels + flevels * count :]

    tm = lax.axis_index("tm")
    freq = lax.axis_index("freq")
    peer = {"tm": 1 - tm}
    sides, partners = [], []
    for j in range(flevels):
        stride = 2**j
        side = (freq // stride) % 2
        sides.append(side)
        partners.append({"freq": freq + stride - 2 * stride * side})

    barrier = pltpu.get_barrier_semaphore()
    for other in [peer] + partners:
        pl.semaphore_signal(barrier, inc=1, device_id=other, device_id_type=MESH)

    lane = lax.broadcasted_iota(jnp.int32, (SUB, LANES), 1)

    for g in range(groups):
        block = x_ref[pl.ds(g * chunks * SUB, chunks * SUB), :].reshape(chunks, SUB, LANES)
        mean = jnp.sum(jnp.sum(block, axis=0), axis=1, keepdims=True) / samples
        off = block - mean[None]
        square = jnp.sum(jnp.sum(off * off, axis=0), axis=1, keepdims=True)
        st_own[0, pl.ds(g * SUB, SUB), :] = jnp.broadcast_to(mean, (SUB, LANES))
        st_own[1, pl.ds(g * SUB, SUB), :] = jnp.broadcast_to(square, (SUB, LANES))

    pl.semaphore_wait(barrier, 1 + flevels)
    stat_copy = pltpu.make_async_remote_copy(
        src_ref=st_own, dst_ref=st_peer, send_sem=ssend, recv_sem=srecv,
        device_id=peer, device_id_type=MESH,
    )
    stat_copy.start()
    halo_copies = []
    for g in range(groups):
        copy = pltpu.make_async_remote_copy(
            src_ref=x_ref.at[pl.ds(g * chunks * SUB, halo_chunks * SUB), :],
            dst_ref=halo.at[g],
            send_sem=hsend.at[g], recv_sem=hrecv.at[g],
            device_id=peer, device_id_type=MESH,
        )
        copy.start()
        halo_copies.append(copy)

    before = lax.broadcasted_iota(jnp.int32, (LANES, 2 * LANES), 0)
    after = lax.broadcasted_iota(jnp.int32, (LANES, 2 * LANES), 1)
    tri[...] = jnp.where(before < after, 1.0, 0.0)
    norm = 1.0 / math.sqrt(channels * freq_count)
    for i in range(nwidth):
        wide = jnp.full((SUB, LANES), w_ref[i].astype(jnp.float32), jnp.float32)
        scl[i] = (1.0 / jnp.sqrt(wide)) * norm

    stat_copy.wait_recv()
    mean_a, mean_b = st_own[0], st_peer[0]
    gap = mean_a - mean_b
    variance = (st_own[1] + st_peer[1] + gap * gap * (samples / 2)) / (2 * samples)
    nrm[0] = (mean_a + mean_b) * 0.5
    nrm[1] = 1.0 / jnp.sqrt(variance + EPSILON)
    for copy in halo_copies:
        copy.wait_recv()

    keep = jnp.where(tm == 0, 1.0, 0.0)

    def rows(body):
        def step(g, carry):
            body(g)
            return carry

        lax.fori_loop(0, groups, step, 0)

    def normalise(c0, size, is_halo):
        def body(g):
            out = []
            for i in range(SUB):
                r = g * SUB + i
                if is_halo:
                    part = halo[g, pl.ds(i, halo_chunks, stride=SUB), :]
                    gain = nrm[1, pl.ds(r, 1), :] * keep
                else:
                    part = x_ref[pl.ds(g * chunks * SUB + c0 * SUB + i, size, stride=SUB), :]
                    gain = nrm[1, pl.ds(r, 1), :]
                out.append((part - nrm[0, pl.ds(r, 1), :]) * gain)
            for i in range(SUB):
                r = g * SUB + i
                count = halo_chunks if is_halo else size
                loc[0][r, pl.ds(c0, count), :] = out[i]

        rows(body)

    def merged(low, high, lag, span, c0, size):
        if span < LANES:
            jump = 0
        else:
            jump = lag // LANES
            lag = lag % LANES
        cur = high(c0 + jump, size)
        nxt = high(c0 + jump + 1, size)
        lanes = lax.broadcasted_iota(jnp.int32, (size, LANES), 1)
        mixed = jnp.where(lanes < lag, nxt, cur)
        return low(c0, size) + pltpu.roll(mixed, (LANES - lag) % LANES, 1)

    def put(level, k, r, rel, size, value):
        bufs[level][k][sides[level], r, pl.ds(rel, size), :] = value

    def local_level(s, k, c0, size):
        span = 2**s
        src = loc[s]

        def body(g):
            out = []
            for i in range(SUB):
                r = g * SUB + i
                base = (r // (2 * span)) * (2 * span)
                lo_row = base + ld_ref[s, 0, r]
                hi_row = base + span + ld_ref[s, 1, r]
                out.append(merged(
                    lambda c, n: src[lo_row, pl.ds(c, n), :],
                    lambda c, n: src[hi_row, pl.ds(c, n), :],
                    ld_ref[s, 2, r], span, c0, size,
                ))
            for i in range(SUB):
                r = g * SUB + i
                if s + 1 < llevels:
                    loc[s + 1][r, pl.ds(c0, size), :] = out[i]
                else:
                    put(0, k, r, c0 - pieces[k][0], size, out[i])

        rows(body)

    def merge_level(j, k, c0, size):
        span = channels * 2**j
        src = bufs[j][k]

        def body(g):
            out = []
            for i in range(SUB):
                r = g * SUB + i
                lo_row = md_ref[j, 0, r]
                hi_row = md_ref[j, 1, r]
                out.append(merged(
                    lambda c, n: src[0, lo_row, pl.ds(c, n), :],
                    lambda c, n: src[1, hi_row, pl.ds(c, n), :],
                    md_ref[j, 2, r], span, c0, size,
                ))
            for i in range(SUB):
                r = g * SUB + i
                if j + 1 < flevels:
                    put(j + 1, k, r, c0, size, out[i])
                else:
                    fin[pl.ds(pl.multiple_of(r * SUB, SUB), SUB), :] = out[i]

        rows(body)

    def prefix(c0):
        sums = jnp.dot(
            fin[...], tri[...], precision=lax.Precision.HIGHEST,
            preferred_element_type=jnp.float32,
        )
        own = sums[:, :LANES].reshape(channels, SUB, LANES)
        eb[:, pl.ds(c0, SUB), :] = own
        return own, sums[:, LANES:].reshape(channels, SUB, LANES)

    def boxcar(c0):
        own, total = prefix(c0)
        far = total + eb[:, pl.ds(c0 + 1, SUB), :]
        lanes = lax.broadcasted_iota(jnp.int32, (channels, SUB, LANES), 2)

        def body(i, best):
            wide = w_ref[i]
            mixed = jnp.where(lanes < wide, far, own)
            ahead = pltpu.roll(mixed, LANES - wide, 2)
            return jnp.maximum(best, (ahead - own) * scl[i][None])

        best = lax.fori_loop(
            0, nwidth, body, jnp.full((channels, SUB, LANES), -jnp.inf, jnp.float32)
        )
        for r in range(channels):
            at = (r // SUB) * chunks * SUB + c0 * SUB + r % SUB
            o_ref[pl.ds(at, SUB, stride=SUB), :] = best[r]

    halo_size = -(-halo_chunks // SUB) * SUB
    pieces = [(chunks - tile * (k + 1), tile) for k in range(count)]

    def tiles(k):
        found = [(pieces[k][0], tile, False)]
        if k == 0:
            found.insert(0, (chunks, halo_size, True))
        return found

    copies = {}
    for j in range(flevels):
        for k in range(count):
            size = tile
            if k == 0:
                size = size + halo_chunks
            window = bufs[j][k].at[sides[j], :, pl.ds(0, size), :]
            copies[j, k] = pltpu.make_async_remote_copy(
                src_ref=window, dst_ref=window,
                send_sem=bsend.at[j, k], recv_sem=brecv.at[j, k],
                device_id=partners[j], device_id_type=MESH,
            )

    def local_stage(k):
        for c0, size, is_halo in tiles(k):
            normalise(c0, size, is_halo)
            for s in range(llevels):
                local_level(s, k, c0, size)
        copies[0, k].start()

    def merge_stage(j, k):
        copies[j, k].wait_recv()
        if k:
            over = channels * 2**j // LANES + 1
            bufs[j][k][:, :, pl.ds(tile, over), :] = bufs[j][k - 1][:, :, pl.ds(0, over), :]
        for c0, size, is_halo in tiles(k):
            rel = c0 - pieces[k][0]
            if j + 1 < flevels:
                merge_level(j, k, rel, size)
            elif is_halo:
                merge_level(j, k, rel, SUB)
                prefix(c0)
            else:
                for sub in reversed(range(size // SUB)):
                    merge_level(j, k, rel + sub * SUB, SUB)
                    boxcar(c0 + sub * SUB)
        if j + 1 < flevels:
            copies[j + 1, k].start()

    lags = [FIRST_LAG] + [MID_LAG] * (flevels - 2) + [LAST_LAG]
    behind = [sum(lags[: j + 1]) for j in range(flevels)]
    for step in range(count + behind[-1]):
        if step < count:
            local_stage(step)
        for j in range(flevels):
            if 0 <= step - behind[j] < count:
                merge_stage(j, step - behind[j])

    stat_copy.wait_send()
    for copy in halo_copies:
        copy.wait_send()
    for copy in copies.values():
        copy.wait_send()


def per_device(mesh_shape, spectra, local_delays, merge_delays, widths):
    channels, block_len = spectra.shape
    freq_count = mesh_shape["freq"]
    chunks = block_len // LANES
    groups = channels // SUB
    tile = SUB
    halo_chunks = -(-(channels * freq_count - 1 + LANES) // LANES)
    halo_size = -(-halo_chunks // SUB) * SUB
    over = -(-(channels * freq_count // 2 // LANES + 1) // SUB) * SUB
    depth = chunks + halo_size + SUB
    llevels = channels.bit_length() - 1
    flevels = freq_count.bit_length() - 1
    count = chunks // tile
    f32 = jnp.float32
    flat = spectra.reshape(groups, SUB, chunks, LANES).transpose(0, 2, 1, 3)
    flat = flat.reshape(groups * chunks * SUB, LANES)
    smem = pl.BlockSpec(memory_space=pltpu.SMEM)
    vmem = pl.BlockSpec(memory_space=pltpu.VMEM)
    dma = pltpu.SemaphoreType.DMA
    out = pl.pallas_call(
        functools.partial(kernel, (channels, chunks, freq_count, halo_chunks, tile)),
        out_shape=jax.ShapeDtypeStruct(flat.shape, f32),
        in_specs=[vmem, smem, smem, smem],
        out_specs=vmem,
        scratch_shapes=[
            pltpu.VMEM((groups, halo_chunks * SUB, LANES), f32),
            pltpu.VMEM((2, channels, LANES), f32),
            pltpu.VMEM((2, channels, LANES), f32),
            pltpu.VMEM((2, channels, LANES), f32),
            pltpu.VMEM((channels * SUB, LANES), f32),
            pltpu.VMEM((channels, depth, LANES), f32),
            pltpu.VMEM((LANES, 2 * LANES), f32),
            pltpu.VMEM((widths.shape[0], SUB, LANES), f32),
        ]
        + [pltpu.VMEM((channels, depth, LANES), f32)] * llevels
        + ([pltpu.VMEM((2, channels, tile + halo_size + over, LANES), f32)]
           + [pltpu.VMEM((2, channels, tile + over, LANES), f32)] * (count - 1)) * flevels
        + [
            dma((groups,)), dma((groups,)), dma, dma,
            dma((flevels, count)), dma((flevels, count)),
        ],
        compiler_params=pltpu.CompilerParams(
            collective_id=0, has_side_effects=True, vmem_limit_bytes=56 * 2**20
        ),
    )(flat, local_delays, merge_delays, widths)
    out = out.reshape(groups, chunks, SUB, LANES).transpose(0, 2, 1, 3)
    return out.reshape(channels, block_len)


def solution(mesh):
    placed = (P(("beam", "freq"), "tm"), P(None, None, "freq"), P(None, None, "freq"), P())
    return jax.shard_map(
        functools.partial(per_device, dict(mesh.shape)), mesh=mesh, in_specs=placed,
        out_specs=P(("beam", "freq"), "tm"), check_vma=False,
    )
```

time: 107 us -> 54.4 us (0.51)
  Pallas kernels: 0 us -> 51 us
  waiting for transfers between devices: 42.1 us -> 0 us
  other arithmetic: 34.5 us -> 0 us
  local copies, waits for them, and re-layouts: 15.3 us -> 3.16 us
  starting transfers between devices: 8.67 us -> 0 us
  blocking collectives: 5.09 us -> 0 us
    pallas_call x0 -> x1, Pallas kernels: none -> 51 us  [per_device(): pl.pallas_call(functools.partial(kernel, (channels, chunks, freq_count, h...]
    ppermute x4 -> x0, waiting for transfers between devices: 42.1 us -> none  [the longest x3 40.5 us: partner_2(): return lax.ppermute(value, axis, pairs)]
    mul x1 -> x0, other arithmetic: 25.4 us -> none  [per_device(): return strongest * (1.0 / math.sqrt(channels * freq_count))]
    gather x20 -> x0, local copies, waits for them, and re-layouts: 14.6 us -> none  [the longest x6 4.39 us: per_device(): low_rows = jnp.where(is_upper, partner[low_pick], series[low_pick])]
    ppermute x4 -> x0, starting transfers between devices: 8.67 us -> none  [the longest x3 7.38 us: partner_2(): return lax.ppermute(value, axis, pairs)]
    psum x2 -> x0, blocking collectives: 5.09 us -> none  [the longest x1 2.62 us: per_device(): totals = lax.psum(jnp.sum(spectra, axis=1, keepdims=True), 'tm')]
    select_n x26 -> x0, other arithmetic: 4.53 us -> none  [the longest x21 4.32 us: shift_rows(): jnp.where(taken, current[:, step:step + new_len], current[:, :new_len])]
    unnamed x8 -> x2, local copies, waits for them, and re-layouts: 0.67 us -> 3.16 us
  transfers between devices with their start and end apart: 4 -> 0, of which waited for: 4 -> 0; matrix products, arithmetic and copies ran while one was open for 5% -> 0% of each run, Pallas kernels for 0% -> 0%
where the time goes in v1:
time: 54.4 us; the launch traced here: 54.1 us
  Pallas kernels  51 us (94%)
  local copies, waits for them, and re-layouts  3.16 us (6%)
    pallas_call x1, Pallas kernels, per_device(): pl.pallas_call(functools.partial(kernel, (channels, chunks, freq_count, h...  51 us
    unnamed x2, local copies, waits for them, and re-layouts  3.16 us

profile of v1, /device:TPU:0, one launch (start us, length us, event | category | flops | bytes accessed | tf_op | source)
XLA Modules:
  0.0 54.1 jit_solution(9249102578219826172)
XLA Ops:
  0.0 1.3 %copy.5.ld_ref = s32[4,3,16]{2,1,0:T(4,128)} copy(s32[4,3,16]{2,0,1:T(4,128)} %param.5) | data formatting | bytes 1536 | tf_op args[1]
  1.3 51.0 %shard_map.46 = f32[1024,128]{1,0:T(8,128)} custom-call(f32[1024,128]{1,0:T(8,128)} %bitcast.11, s32[4,3,16]{2,1,0:T(4,128)} %copy.5.ld_ref, s32[3,3,16]{2,1,0:T(4,128)} %md_ref.1, s32[16]{0:T(128)} %w_ref.1), custom_call_target="tpu_custom_call" | custom-call | tf_op jit(solution)/shard_map/pallas_call | solution.py:295
  52.3 1.9 %copy.7 = f32[16,8192]{1,0:T(8,128)} copy(f32[16,8192]{1,0:T(8,128)} %bitcast.10) | data formatting | bytes 1048576

commit v2 on v1

--- a/solution.py
+++ b/solution.py
@@ -16,6 +16,7 @@
 FIRST_LAG = 1
 MID_LAG = 1
 LAST_LAG = 3
+UNROLL = 16
 
 
 def kernel(geo, x_ref, ld_ref, md_ref, w_ref, o_ref, *scratch):
@@ -93,11 +94,8 @@
     keep = jnp.where(tm == 0, 1.0, 0.0)
 
     def rows(body):
-        def step(g, carry):
+        for g in range(groups):
             body(g)
-            return carry
-
-        lax.fori_loop(0, groups, step, 0)
 
     def normalise(c0, size, is_halo):
         def body(g):
@@ -142,12 +140,12 @@
             for i in range(SUB):
                 r = g * SUB + i
                 base = (r // (2 * span)) * (2 * span)
-                lo_row = base + ld_ref[s, 0, r]
-                hi_row = base + span + ld_ref[s, 1, r]
+                lo_row = base + ld_ref[0, s, r]
+                hi_row = base + span + ld_ref[1, s, r]
                 out.append(merged(
                     lambda c, n: src[lo_row, pl.ds(c, n), :],
                     lambda c, n: src[hi_row, pl.ds(c, n), :],
-                    ld_ref[s, 2, r], span, c0, size,
+                    ld_ref[2, s, r], span, c0, size,
                 ))
             for i in range(SUB):
                 r = g * SUB + i
@@ -196,14 +194,18 @@
         far = total + eb[:, pl.ds(c0 + 1, SUB), :]
         lanes = lax.broadcasted_iota(jnp.int32, (channels, SUB, LANES), 2)
 
-        def body(i, best):
-            wide = w_ref[i]
-            mixed = jnp.where(lanes < wide, far, own)
-            ahead = pltpu.roll(mixed, LANES - wide, 2)
-            return jnp.maximum(best, (ahead - own) * scl[i][None])
-
+        def body(at, best):
+            for u in range(unroll):
+                i = at * unroll + u
+                wide = w_ref[i]
+                mixed = jnp.where(lanes < wide, far, own)
+                ahead = pltpu.roll(mixed, LANES - wide, 2)
+                best = jnp.maximum(best, (ahead - own) * scl[i][None])
+            return best
+
+        unroll = math.gcd(nwidth, UNROLL)
         best = lax.fori_loop(
-            0, nwidth, body, jnp.full((channels, SUB, LANES), -jnp.inf, jnp.float32)
+            0, nwidth // unroll, body, jnp.full((channels, SUB, LANES), -jnp.inf, jnp.float32)
         )
         for r in range(channels):
             at = (r // SUB) * chunks * SUB + c0 * SUB + r % SUB
@@ -317,7 +319,7 @@
         compiler_params=pltpu.CompilerParams(
             collective_id=0, has_side_effects=True, vmem_limit_bytes=56 * 2**20
         ),
-    )(flat, local_delays, merge_delays, widths)
+    )(flat, local_delays.transpose(1, 0, 2), merge_delays, widths)
     out = out.reshape(groups, chunks, SUB, LANES).transpose(0, 2, 1, 3)
     return out.reshape(channels, block_len)
 

time: 54.4 us -> 44.2 us (0.81)
  Pallas kernels: 51 us -> 42.2 us
  local copies, waits for them, and re-layouts: 3.16 us -> 1.87 us
    pallas_call x1, Pallas kernels: 51 us -> 42.2 us  [per_device(): pl.pallas_call(functools.partial(kernel, (channels, chunks, freq_count, h...]
    unnamed x2 -> x1, local copies, waits for them, and re-layouts: 3.16 us -> 1.87 us
where the time goes in v2:
time: 44.2 us; the launch traced here: 44.1 us
  Pallas kernels  42.2 us (95%)
  local copies, waits for them, and re-layouts  1.87 us (4%)
    pallas_call x1, Pallas kernels, per_device(): pl.pallas_call(functools.partial(kernel, (channels, chunks, freq_count, h...  42.2 us
    unnamed x1, local copies, waits for them, and re-layouts  1.87 us

profile of v2, /device:TPU:0, one launch (start us, length us, event | category | flops | bytes accessed | tf_op | source)
XLA Modules:
  0.0 44.1 jit_solution(16704687297345605323)
XLA Ops:
  0.0 42.2 %shard_map.46 = f32[1024,128]{1,0:T(8,128)} custom-call(f32[1024,128]{1,0:T(8,128)} %bitcast.12, s32[3,4,16]{2,1,0:T(4,128)} %bitcast.13, s32[3,3,16]{2,1,0:T(4,128)} %md_ref.1, s32[16]{0:T(128)} %w_ref.1), custom_call_target="tpu_custom_call" | custom-call | tf_op jit(solution)/shard_map/pallas_call | solution.py:297
  42.2 1.9 %copy.6 = f32[16,8192]{1,0:T(8,128)} copy(f32[16,8192]{1,0:T(8,128)} %bitcast.11) | data formatting | bytes 1048576

commit v3 on v2

--- a/solution.py
+++ b/solution.py
@@ -296,7 +296,7 @@
     dma = pltpu.SemaphoreType.DMA
     out = pl.pallas_call(
         functools.partial(kernel, (channels, chunks, freq_count, halo_chunks, tile)),
-        out_shape=jax.ShapeDtypeStruct(flat.shape, f32),
+        out_shape=pltpu.VMEM(flat.shape, f32),
         in_specs=[vmem, smem, smem, smem],
         out_specs=vmem,
         scratch_shapes=[

time: 44.2 us -> 42.3 us (0.957)
  local copies, waits for them, and re-layouts: 1.87 us -> 0.8 us
  Pallas kernels: 42.2 us -> 41.4 us
    unnamed x1, local copies, waits for them, and re-layouts: 1.87 us -> 0.8 us
    pallas_call x1, Pallas kernels: 42.2 us -> 41.4 us  [per_device(): pl.pallas_call(functools.partial(kernel, (channels, chunks, freq_count, h...]
where the time goes in v3:
time: 42.3 us; the launch traced here: 42.2 us
  Pallas kernels  41.4 us (98%)
  local copies, waits for them, and re-layouts  0.8 us (2%)
    pallas_call x1, Pallas kernels, per_device(): pl.pallas_call(functools.partial(kernel, (channels, chunks, freq_count, h...  41.4 us

profile of v3, /device:TPU:0, one launch (start us, length us, event | category | flops | bytes accessed | tf_op | source)
XLA Modules:
  0.0 42.2 jit_solution(13077965989395054019)
XLA Ops:
  0.0 41.4 %shard_map.46 = f32[1024,128]{1,0:T(8,128)S(1)} custom-call(f32[1024,128]{1,0:T(8,128)} %bitcast.12, s32[3,4,16]{2,1,0:T(4,128)} %bitcast.13, s32[3,3,16]{2,1,0:T(4,128)} %md_ref.1, s32[16]{0:T(128)} %w_ref.1), custom_call_target="tpu_custom_call" | custom-call | tf_op jit(solution)/shard_map/pallas_call | solution.py:297
  41.4 0.8 %copy.6 = f32[16,8192]{1,0:T(8,128)} copy(f32[16,8192]{1,0:T(8,128)S(1)} %bitcast.11) | data formatting | bytes 1048576
